TPU v7x, 32 devices: a whole 2x2x4 slice. The times are simulated.
32 devices in a mesh: img: 4 (over x, core), tok: 8 (over z, y).
Axes of the slice: x: 2, y: 2, z: 4, core: 2. Of those that a mesh axis runs over, the one named last changes fastest.
Arguments:
- student: bfloat16 [4, 1024, 4096], P('img', None, 'tok'), may hold values from -0.32 to 0.32
- teacher: bfloat16 [4, 64, 64, 4096], P('img', None, None, 'tok'), may hold values from -160 to 160
Outputs:
- gradient: bfloat16 [4, 1024, 4096], P('img', None, 'tok')
- loss: float32 [], replicated
All inputs are finite; a program needn't handle non-finite values.
Results may differ from a plain program's by a relative error of at most 0.0069.
Values may be sent and summed in bfloat16 or wider, within the bound.
A program may use at most 64 MiB of HBM per device.

v0:
```python
import functools

import jax
import jax.numpy as jnp
import numpy as np
from jax import lax
from jax.experimental import pallas as pl
from jax.experimental.pallas import tpu as pltpu
from jax.sharding import PartitionSpec as P

cubic_taps = (-0.09375, 0.59375, 0.59375, -0.09375)
epsilon = 1e-06
LANES = 128
BLOCK = 256
SPLIT = 2
LAG = 2


def lane_tiles_sum(x):
    total = x[:, :LANES]
    for start in range(LANES, x.shape[1], LANES):
        total = total + x[:, start : start + LANES]
    return total


def spread(column, width):
    return jnp.concatenate([column] * (width // LANES), axis=1)


def kernel(
    sizes, student_hbm, teacher_hbm, taps_ref, out_ref, loss_ref,
    sbuf, tbuf, hbuf, shrunk, unit_low, teach_low, part, inv, tinv,
    snorm, tnorm, along, losses, img_losses,
    own, prefix, theirs, ysend, yrecv, zin, zout, mlow, pull, sqacc,
    load_sem, s_send, s_recv, t_send, t_recv, a_send, a_recv, l_send, l_recv,
    i_send, i_recv, y_send, y_recv, z_send, z_recv, g_send, g_recv,
):
    n, m = sizes
    tokens, feats = unit_low.shape
    height, width = tbuf.shape[0], tbuf.shape[1]
    group = load_sem.shape[0] - 1
    rows_per = height // group
    half_w = width // 2
    nb = tokens // BLOCK
    tiles = tokens // LANES
    me = lax.axis_index("tok")
    img = lax.axis_index("img")
    col = lax.rem(me, 2)
    row = me // 2
    chain = n // 2
    square = [(i, i) for i in range(nb)]
    upper = [(i, j) for i in range(nb) for j in range(i + 1, nb)]
    diag, off = len(square) // 2, len(upper) // 2
    pairs = upper[:off] + square[:diag] + upper[off:] + square[diag:]
    half = diag + off
    count = half * SPLIT
    depth = BLOCK // SPLIT
    early = jnp.where(row < (chain + 1) // 2, 0, 1)
    late = 1 - early
    rank = jnp.minimum(row, chain - 1 - row)

    def load(g):
        rows = pl.ds(g * rows_per, rows_per)
        return pltpu.make_async_copy(
            teacher_hbm.at[0, rows], tbuf.at[rows], load_sem.at[g]
        )

    student_load = pltpu.make_async_copy(student_hbm.at[0], sbuf, load_sem.at[group])
    student_load.start()

    @pl.loop(0, group)
    def _(g):
        load(g).start()

    barrier = pltpu.get_barrier_semaphore()
    for p in range(1, n):
        pl.semaphore_signal(barrier, 1, device_id={"tok": lax.rem(me + p, n)})
    for p in range(1, m):
        pl.semaphore_signal(barrier, 1, device_id={"img": lax.rem(img + p, m)})

    def gather_copies(buf, send, recv, axis, here, size):
        return [
            pltpu.make_async_remote_copy(
                src_ref=buf.at[here],
                dst_ref=buf.at[here],
                send_sem=send.at[p - 1],
                recv_sem=recv.at[p - 1],
                device_id={axis: lax.rem(here + p, size)},
            )
            for p in range(1, size)
        ]

    def pack_rows(buf):
        @pl.loop(0, tiles)
        def _(b):
            block = part[pl.ds(pl.multiple_of(b * LANES, LANES), LANES), :]
            buf[me, pl.ds(b, 1), :] = jnp.sum(block.T, axis=0, keepdims=True)

    def summed(buf, size):
        total = buf[0]
        for k in range(1, size):
            total = total + buf[k]
        return total

    def unpack_rows(values, dst):
        for b in range(tiles):
            dst[b * LANES : (b + 1) * LANES, :] = jnp.broadcast_to(
                values[b : b + 1, :], (LANES, LANES)
            ).T

    def slab(b):
        return pl.ds(pl.multiple_of(b * LANES, LANES), LANES)

    @pl.when(rank == 0)
    def _():
        zin[early] = jnp.zeros(zin.shape[1:], zin.dtype)

    sqacc[...] = jnp.zeros_like(sqacc)
    student_load.wait()

    @pl.loop(0, tiles)
    def _(b):
        x = sbuf[slab(b), :].astype(jnp.float32)
        part[slab(b), :] = lane_tiles_sum(x * x)

    pack_rows(snorm)
    @pl.loop(0, group)
    def _(g):
        load(g).wait()
        x = tbuf[pl.ds(g * rows_per, rows_per)].reshape(rows_per * width, feats)
        y = jnp.dot(taps_ref[...], x, preferred_element_type=jnp.float32)
        hbuf[pl.ds(g * rows_per + 1, rows_per)] = y.reshape(rows_per, half_w, feats)

    pl.semaphore_wait(barrier, n - 1 + m - 1)
    s_copies = gather_copies(snorm, s_send, s_recv, "tok", me, n)
    for copy in s_copies:
        copy.start()

    hbuf[0] = hbuf[1]
    hbuf[height + 1] = hbuf[height]

    @pl.loop(0, height // 2)
    def _(a):
        v = cubic_taps[0] * hbuf[2 * a]
        for k in range(1, 4):
            v = v + cubic_taps[k] * hbuf[2 * a + k]
        rows = pl.ds(pl.multiple_of(a * half_w, half_w), half_w)
        shrunk[rows, :] = v
        part[rows, :] = lane_tiles_sum(v * v)

    pack_rows(tnorm)
    t_copies = gather_copies(tnorm, t_send, t_recv, "tok", me, n)
    for copy in t_copies:
        copy.start()

    for copy in s_copies:
        copy.wait_recv()
    unpack_rows(lax.rsqrt(summed(snorm, n) + epsilon), inv)

    @pl.loop(0, tiles)
    def _(b):
        x = sbuf[slab(b), :].astype(jnp.float32) * spread(inv[slab(b), :], feats)
        unit_low[slab(b), :] = x.astype(jnp.bfloat16)

    def pick(k, c):
        first, second = pairs[k], pairs[half + k]
        i = first[0] + c * (second[0] - first[0])
        j = first[1] + c * (second[1] - first[1])
        return i, j

    def strip(i):
        return pl.ds(pl.multiple_of(i * BLOCK, BLOCK), BLOCK)

    def gram(low, i, j):
        return lax.dot_general(
            low[strip(i), :], low[strip(j), :], (((1,), (1,)), ((), ())),
            preferred_element_type=jnp.float32,
        )

    for k in range(half):
        theirs[k] = gram(unit_low, *pick(k, 1 - col))
    for k in range(half):
        pieces = gram(unit_low, *pick(k, col))
        own[k * SPLIT : (k + 1) * SPLIT] = pieces.reshape(SPLIT, depth, BLOCK)

    for copy in t_copies:
        copy.wait_recv()
    unpack_rows(lax.rsqrt(summed(tnorm, n) + epsilon), tinv)

    @pl.loop(0, tiles)
    def _(b):
        x = shrunk[slab(b), :] * spread(tinv[slab(b), :], feats)
        teach_low[slab(b), :] = x.astype(jnp.bfloat16)

    def skip(k):
        return (k % SPLIT) * depth if k >= off * SPLIT else 0

    y_copies = []
    for k in range(half):
        d = theirs[k] - gram(teach_low, *pick(k, 1 - col))
        pieces = d.astype(jnp.bfloat16).reshape(SPLIT, depth, BLOCK)
        ysend[k * SPLIT : (k + 1) * SPLIT] = pieces
        for t in range(k * SPLIT, (k + 1) * SPLIT):
            copy = pltpu.make_async_remote_copy(
                src_ref=ysend.at[t, :, skip(t) :], dst_ref=yrecv.at[t, :, skip(t) :],
                send_sem=y_send.at[t], recv_sem=y_recv.at[t],
                device_id={"tok": me + 1 - 2 * col},
            )
            copy.start()
            y_copies.append(copy)
    for k in range(half):
        d = gram(teach_low, *pick(k, col)).reshape(SPLIT, depth, BLOCK)
        own[k * SPLIT : (k + 1) * SPLIT] = own[k * SPLIT : (k + 1) * SPLIT] - d

    def chain_copy(direction, k):
        step = 2 - 4 * direction
        return pltpu.make_async_remote_copy(
            src_ref=zout.at[direction, k, :, skip(k) :],
            dst_ref=zin.at[direction, k, :, skip(k) :],
            send_sem=z_send.at[direction, k], recv_sem=z_recv.at[direction, k],
            device_id={"tok": lax.rem(me + step + n, n)},
        )

    def piece(k, c):
        i, j = pick(k // SPLIT, c)
        start = i * BLOCK + (k % SPLIT) * depth
        columns = pl.ds(pl.multiple_of(j * BLOCK + skip(k), depth), BLOCK - skip(k))
        return i, j, pl.ds(pl.multiple_of(start, depth), depth), columns

    def mirror(k, c, block):
        _, j, rows, _ = piece(k, c)
        first = 0
        if k >= off * SPLIT:
            first = skip(k) + depth
            block = block[:, depth:]
        if first < BLOCK:
            start = pl.multiple_of(j * BLOCK + first, depth)
            mlow[pl.ds(start, BLOCK - first), rows] = block.T.astype(jnp.bfloat16)

    def block_copy(k):
        _, _, rows, columns = piece(k, col)
        block = mlow.at[rows, columns]
        return pltpu.make_async_remote_copy(
            src_ref=block, dst_ref=block,
            send_sem=g_send.at[k], recv_sem=g_recv.at[k],
            device_id={"tok": me + 1 - 2 * col},
        )

    def run_early(k):
        y_copies[k].wait_recv()
        cut = skip(k)
        mine = own[k, :, cut:] + yrecv[k, :, cut:].astype(jnp.float32)
        copy = chain_copy(early, k)

        @pl.when(rank > 0)
        def _():
            copy.wait_recv()

        total = mine + zin[early, k, :, cut:].astype(jnp.float32)
        zout[early, k, :, cut:] = total.astype(jnp.bfloat16)
        own[k, :, cut:] = mine
        prefix[k, :, cut:] = total
        copy.start()

    def run_late(k):
        copy = chain_copy(late, k)
        copy.wait_recv()
        cut = skip(k)
        incoming = zin[late, k, :, cut:].astype(jnp.float32)
        total = prefix[k, :, cut:] + incoming
        _, _, rows, columns = piece(k, col)
        low = total.astype(jnp.bfloat16)

        @pl.when(rank > 0)
        def _():
            zout[late, k, :, cut:] = (own[k, :, cut:] + incoming).astype(jnp.bfloat16)
            copy.start()

        mlow[rows, columns] = low
        block_copy(k).start()
        sums = jnp.sum(total * total, axis=0, keepdims=True)
        if k >= off * SPLIT:
            sqacc[:, :depth] += sums[:, :depth]
            if cut + depth < BLOCK:
                sqacc[:, cut + depth :] += 2.0 * sums[:, depth:]
        else:
            sqacc[...] += 2.0 * sums
        mirror(k, col, total)

    def run_chain(lag):
        for t in range(count + lag):
            if t < count:
                run_early(t)
            if t >= lag:
                run_late(t - lag)

    @pl.when(rank == 0)
    def _():
        run_chain(count)

    @pl.when(rank > 0)
    def _():
        run_chain(min(LAG, count))

    squared = jnp.sum(sqacc[...], axis=1, keepdims=True)
    losses[me] = jnp.broadcast_to(squared, losses.shape[1:])
    l_copies = gather_copies(losses, l_send, l_recv, "tok", me, n)
    for copy in l_copies:
        copy.start()

    for k in range(count):
        block_copy(k).wait_recv()
        _, _, rows, columns = piece(k, 1 - col)
        mirror(k, 1 - col, mlow[rows, columns].astype(jnp.float32))

    @pl.loop(0, nb)
    def _(b):
        rows = strip(b)
        p = 4.0 * jnp.dot(mlow[rows, :], unit_low[...], preferred_element_type=jnp.float32)
        pull[rows, :] = p
        unit = sbuf[rows, :].astype(jnp.float32) * spread(inv[rows, :], feats)
        part[rows, :] = lane_tiles_sum(unit * p)

    pack_rows(along)
    a_copies = gather_copies(along, a_send, a_recv, "tok", me, n)
    for copy in a_copies:
        copy.start()

    for copy in l_copies:
        copy.wait_recv()
    img_losses[img] = summed(losses, n)
    i_copies = gather_copies(img_losses, i_send, i_recv, "img", img, m)
    for copy in i_copies:
        copy.start()

    for copy in a_copies:
        copy.wait_recv()
    unpack_rows(summed(along, n), tinv)

    @pl.loop(0, tiles)
    def _(b):
        scale = spread(inv[slab(b), :], feats)
        unit = sbuf[slab(b), :].astype(jnp.float32) * scale
        grad = scale * pull[slab(b), :] - scale * unit * spread(tinv[slab(b), :], feats)
        out_ref[0, slab(b), :] = grad.astype(out_ref.dtype)

    for copy in i_copies:
        copy.wait_recv()
    loss_ref[...] = summed(img_losses, m) / (chain * tokens)

    for copy in s_copies + t_copies + l_copies + a_copies + i_copies + y_copies:
        copy.wait_send()
    for k in range(count):
        block_copy(k).wait_send()
        chain_copy(early, k).wait_send()

        @pl.when(rank > 0)
        def _():
            chain_copy(late, k).wait_send()


def tap_matrix(width, rows_per):
    half = width // 2
    taps = np.zeros((half, width), np.float32)
    for b in range(half):
        for q in range(4):
            taps[b, min(max(2 * b - 1 + q, 0), width - 1)] += cubic_taps[q]
    return jnp.asarray(np.kron(np.eye(rows_per, dtype=np.float32), taps), jnp.bfloat16)


def per_device(n, m, student, teacher):
    _, tokens, feats = student.shape
    _, height, width, _ = teacher.shape
    rows_per = max(1, 256 // width)
    groups = height // rows_per
    nb = tokens // BLOCK
    half = nb // 2 + nb * (nb - 1) // 4
    count = half * SPLIT
    depth = BLOCK // SPLIT
    tiles = tokens // LANES
    f32, bf16 = jnp.float32, jnp.bfloat16
    vmem, dma = pltpu.VMEM, pltpu.SemaphoreType.DMA
    gradient, loss = pl.pallas_call(
        functools.partial(kernel, (n, m)),
        name="anchor",
        out_shape=(
            jax.ShapeDtypeStruct(student.shape, bf16),
            jax.ShapeDtypeStruct((8, LANES), f32),
        ),
        in_specs=[
            pl.BlockSpec(memory_space=pl.ANY),
            pl.BlockSpec(memory_space=pl.ANY),
            pl.BlockSpec(memory_space=pltpu.VMEM),
        ],
        out_specs=(
            pl.BlockSpec(memory_space=pltpu.VMEM),
            pl.BlockSpec(memory_space=pltpu.VMEM),
        ),
        scratch_shapes=[
            vmem((tokens, feats), bf16),
            vmem((height, width, feats), bf16),
            vmem((height + 2, width // 2, feats), f32),
            vmem((tokens, feats), f32),
            vmem((tokens, feats), bf16),
            vmem((tokens, feats), bf16),
            vmem((tokens, LANES), f32),
            vmem((tokens, LANES), f32),
            vmem((tokens, LANES), f32),
            vmem((n, tiles, LANES), f32),
            vmem((n, tiles, LANES), f32),
            vmem((n, tiles, LANES), f32),
            vmem((n, 8, LANES), f32),
            vmem((m, 8, LANES), f32),
            vmem((count, depth, BLOCK), f32),
            vmem((count, depth, BLOCK), f32),
            vmem((half, BLOCK, BLOCK), f32),
            vmem((count, depth, BLOCK), bf16),
            vmem((count, depth, BLOCK), bf16),
            vmem((2, count, depth, BLOCK), bf16),
            vmem((2, count, depth, BLOCK), bf16),
            vmem((tokens, tokens), bf16),
            vmem((tokens, feats), f32),
            vmem((1, BLOCK), f32),
            dma((groups + 1,)),
            dma((n - 1,)), dma((n - 1,)), dma((n - 1,)), dma((n - 1,)),
            dma((n - 1,)), dma((n - 1,)), dma((n - 1,)), dma((n - 1,)),
            dma((m - 1,)), dma((m - 1,)),
            dma((count,)), dma((count,)),
            dma((2, count)), dma((2, count)),
            dma((count,)), dma((count,)),
        ],
        compiler_params=pltpu.CompilerParams(
            collective_id=0, has_side_effects=True, vmem_limit_bytes=56 * 1024 * 1024
        ),
    )(student, teacher, tap_matrix(width, rows_per))
    return gradient, loss[0, 0]


def solution(mesh):
    return jax.shard_map(
        functools.partial(per_device, mesh.shape["tok"], mesh.shape["img"]),
        mesh=mesh,
        in_specs=(P("img", None, "tok"), P("img", None, None, "tok")),
        out_specs=(P("img", None, "tok"), P()),
        check_vma=False,
    )
```

profile of v0, /device:TPU:0, one launch (start us, length us, event | category | flops | bytes accessed | tf_op | source)
XLA Modules:
  0.0 57.9 jit_solution(9911401601273216804)
XLA Ops:
  0.6 53.8 %anchor.1 = (bf16[1,1024,512]{2,1,0:T(8,128)(2,1)}, f32[8,128]{1,0:T(8,128)}) custom-call(bf16[1,1024,512]{2,1,0:T(8,128)(2,1)} %student_hbm.1, bf16[1,64,64,512]{3,2,1,0:T(8,128)(2,1)} %teacher_hbm.1, bf16[128,256]{1,0:T(8,128)(2,1)} %constant.2.clone.taps_ref), custom_call_target="tpu_custom_call" | custom-call | tf_op jit(solution)/shard_map/anchor/pallas_call | solution.py:383
  54.4 1.2 %slice.3 = f32[1,1]{1,0:T(1,128)} slice(f32[8,128]{1,0:T(8,128)} %get-tuple-element.5), slice={[0:1], [0:1]} | slice | bytes 8 | tf_op jit(solution)/shard_map/slice | solution.py:436
  55.6 2.3 %copy.6 = bf16[1,1024,512]{2,1,0:T(8,128)(2,1)} copy(bf16[1,1024,512]{2,1,0:T(8,128)(2,1)} %get-tuple-element.8) | data formatting | bytes 2097152
where the time goes:
time: 58.1 us; the launch traced here: 57.9 us
  Pallas kernels  53.8 us (93%)
  local copies, waits for them, and re-layouts  3.45 us (6%)
  between operations  0.64 us (1%)
    pallas_call x1, Pallas kernels, per_device(): pl.pallas_call(functools.partial(kernel, (n, m)), name='anchor', out_shap...  53.8 us
    unnamed x1, local copies, waits for them, and re-layouts  2.26 us
    slice x1, local copies, waits for them, and re-layouts, per_device(): return (gradient, loss[0, 0])  1.19 us

commit v1 on v0

--- a/solution.py
+++ b/solution.py
@@ -2,7 +2,6 @@
 
 import jax
 import jax.numpy as jnp
-import numpy as np
 from jax import lax
 from jax.experimental import pallas as pl
 from jax.experimental.pallas import tpu as pltpu
@@ -14,6 +13,8 @@
 BLOCK = 256
 SPLIT = 2
 LAG = 2
+CHUNKS = 4
+UNROLL = 2
 
 
 def lane_tiles_sum(x):
@@ -28,19 +29,18 @@
 
 
 def kernel(
-    sizes, student_hbm, teacher_hbm, taps_ref, out_ref, loss_ref,
-    sbuf, tbuf, hbuf, shrunk, unit_low, teach_low, part, inv, tinv,
-    snorm, tnorm, along, losses, img_losses,
+    sizes, student_hbm, teacher_hbm, out_ref, loss_ref,
+    sbuf, tbuf, vbuf, shrunk, unit_low, teach_low, part, tpart, inv, tinv,
+    norms, along, losses, img_losses,
     own, prefix, theirs, ysend, yrecv, zin, zout, mlow, pull, sqacc,
-    load_sem, s_send, s_recv, t_send, t_recv, a_send, a_recv, l_send, l_recv,
+    load_sem, s_send, s_recv, a_send, a_recv, l_send, l_recv,
     i_send, i_recv, y_send, y_recv, z_send, z_recv, g_send, g_recv,
 ):
     n, m = sizes
     tokens, feats = unit_low.shape
-    height, width = tbuf.shape[0], tbuf.shape[1]
-    group = load_sem.shape[0] - 1
-    rows_per = height // group
+    height, width = tbuf.shape[0] - 2, tbuf.shape[1]
     half_w = width // 2
+    lane_tiles = feats // LANES
     nb = tokens // BLOCK
     tiles = tokens // LANES
     me = lax.axis_index("tok")
@@ -59,18 +59,26 @@
     late = 1 - early
     rank = jnp.minimum(row, chain - 1 - row)
 
-    def load(g):
-        rows = pl.ds(g * rows_per, rows_per)
-        return pltpu.make_async_copy(
-            teacher_hbm.at[0, rows], tbuf.at[rows], load_sem.at[g]
+    student_load = pltpu.make_async_copy(student_hbm.at[0], sbuf, load_sem.at[0])
+    student_load.start()
+
+    def load(index, first, last, to):
+        copy = pltpu.make_async_copy(
+            teacher_hbm.at[0, first:last],
+            tbuf.at[to : to + last - first],
+            load_sem.at[index],
         )
-
-    student_load = pltpu.make_async_copy(student_hbm.at[0], sbuf, load_sem.at[group])
-    student_load.start()
-
-    @pl.loop(0, group)
-    def _(g):
-        load(g).start()
+        copy.start()
+        return copy
+
+    step = height // CHUNKS
+    top = load(1, 0, 1, 0)
+    loads = []
+    for q in range(CHUNKS):
+        first = q * step + 1 if q else 0
+        last = height if q == CHUNKS - 1 else (q + 1) * step + 1
+        loads.append(load(3 + q, first, last, first + 1))
+    bottom = load(2, height - 1, height, height + 1)
 
     barrier = pltpu.get_barrier_semaphore()
     for p in range(1, n):
@@ -90,11 +98,15 @@
             for p in range(1, size)
         ]
 
-    def pack_rows(buf):
-        @pl.loop(0, tiles)
-        def _(b):
-            block = part[pl.ds(pl.multiple_of(b * LANES, LANES), LANES), :]
-            buf[me, pl.ds(b, 1), :] = jnp.sum(block.T, axis=0, keepdims=True)
+    def pack_rows(sources):
+        lane = lax.broadcasted_iota(jnp.int32, (LANES, LANES), 1)
+        columns = jnp.zeros((LANES, LANES), jnp.float32)
+        for k, source in enumerate(sources):
+            for b in range(tiles):
+                block = source[b * LANES : (b + 1) * LANES, :]
+                total = jnp.sum(block, axis=1, keepdims=True)
+                columns = jnp.where(lane == k * tiles + b, total, columns)
+        return columns.T[: len(sources) * tiles]
 
     def summed(buf, size):
         total = buf[0]
@@ -102,11 +114,15 @@
             total = total + buf[k]
         return total
 
-    def unpack_rows(values, dst):
-        for b in range(tiles):
-            dst[b * LANES : (b + 1) * LANES, :] = jnp.broadcast_to(
-                values[b : b + 1, :], (LANES, LANES)
-            ).T
+    def unpack_rows(values, targets):
+        blank = jnp.zeros((LANES - values.shape[0], LANES), jnp.float32)
+        columns = jnp.concatenate([values, blank], axis=0).T
+        for k, target in enumerate(targets):
+            for b in range(tiles):
+                at = k * tiles + b
+                target[b * LANES : (b + 1) * LANES, :] = jnp.broadcast_to(
+                    columns[:, at : at + 1], (LANES, LANES)
+                )
 
     def slab(b):
         return pl.ds(pl.multiple_of(b * LANES, LANES), LANES)
@@ -123,39 +139,43 @@
         x = sbuf[slab(b), :].astype(jnp.float32)
         part[slab(b), :] = lane_tiles_sum(x * x)
 
-    pack_rows(snorm)
-    @pl.loop(0, group)
-    def _(g):
-        load(g).wait()
-        x = tbuf[pl.ds(g * rows_per, rows_per)].reshape(rows_per * width, feats)
-        y = jnp.dot(taps_ref[...], x, preferred_element_type=jnp.float32)
-        hbuf[pl.ds(g * rows_per + 1, rows_per)] = y.reshape(rows_per, half_w, feats)
-
+    def shrink_pair(first):
+        for u in range(UNROLL):
+            a = first * UNROLL + u
+            x = [tbuf[2 * a + k].astype(jnp.float32) for k in range(4)]
+            v = cubic_taps[1] * (x[1] + x[2]) + cubic_taps[0] * (x[0] + x[3])
+            for t in range(lane_tiles):
+                tile = v[:, t * LANES : (t + 1) * LANES]
+                vbuf[u, t, 8 : 8 + width, :] = tile
+                vbuf[u, t, 7:8, :] = tile[0:1]
+                vbuf[u, t, 8 + width : 9 + width, :] = tile[width - 1 : width]
+        for u in range(UNROLL):
+            a = first * UNROLL + u
+            rows = pl.ds(pl.multiple_of(a * half_w, half_w), half_w)
+            total = None
+            for t in range(lane_tiles):
+                w = [vbuf[u, t, pl.ds(7 + k, half_w, stride=2), :] for k in range(4)]
+                h = cubic_taps[1] * (w[1] + w[2]) + cubic_taps[0] * (w[0] + w[3])
+                shrunk[rows, t * LANES : (t + 1) * LANES] = h
+                total = h * h if total is None else total + h * h
+            tpart[rows, :] = total
+
+    top.wait()
+    for q in range(CHUNKS):
+        loads[q].wait()
+        if q == CHUNKS - 1:
+            bottom.wait()
+        trips = step // 2 // UNROLL
+        pl.loop(q * trips, (q + 1) * trips)(shrink_pair)
+
+    norms[me] = pack_rows((part, tpart))
     pl.semaphore_wait(barrier, n - 1 + m - 1)
-    s_copies = gather_copies(snorm, s_send, s_recv, "tok", me, n)
+    s_copies = gather_copies(norms, s_send, s_recv, "tok", me, n)
     for copy in s_copies:
         copy.start()
-
-    hbuf[0] = hbuf[1]
-    hbuf[height + 1] = hbuf[height]
-
-    @pl.loop(0, height // 2)
-    def _(a):
-        v = cubic_taps[0] * hbuf[2 * a]
-        for k in range(1, 4):
-            v = v + cubic_taps[k] * hbuf[2 * a + k]
-        rows = pl.ds(pl.multiple_of(a * half_w, half_w), half_w)
-        shrunk[rows, :] = v
-        part[rows, :] = lane_tiles_sum(v * v)
-
-    pack_rows(tnorm)
-    t_copies = gather_copies(tnorm, t_send, t_recv, "tok", me, n)
-    for copy in t_copies:
-        copy.start()
-
     for copy in s_copies:
         copy.wait_recv()
-    unpack_rows(lax.rsqrt(summed(snorm, n) + epsilon), inv)
+    unpack_rows(lax.rsqrt(summed(norms, n) + epsilon), (inv, tinv))
 
     @pl.loop(0, tiles)
     def _(b):
@@ -182,10 +202,6 @@
     for k in range(half):
         pieces = gram(unit_low, *pick(k, col))
         own[k * SPLIT : (k + 1) * SPLIT] = pieces.reshape(SPLIT, depth, BLOCK)
-
-    for copy in t_copies:
-        copy.wait_recv()
-    unpack_rows(lax.rsqrt(summed(tnorm, n) + epsilon), tinv)
 
     @pl.loop(0, tiles)
     def _(b):
@@ -321,7 +337,7 @@
         unit = sbuf[rows, :].astype(jnp.float32) * spread(inv[rows, :], feats)
         part[rows, :] = lane_tiles_sum(unit * p)
 
-    pack_rows(along)
+    along[me] = pack_rows((part,))
     a_copies = gather_copies(along, a_send, a_recv, "tok", me, n)
     for copy in a_copies:
         copy.start()
@@ -335,7 +351,7 @@
 
     for copy in a_copies:
         copy.wait_recv()
-    unpack_rows(summed(along, n), tinv)
+    unpack_rows(summed(along, n), (tinv,))
 
     @pl.loop(0, tiles)
     def _(b):
@@ -348,7 +364,7 @@
         copy.wait_recv()
     loss_ref[...] = summed(img_losses, m) / (chain * tokens)
 
-    for copy in s_copies + t_copies + l_copies + a_copies + i_copies + y_copies:
+    for copy in s_copies + l_copies + a_copies + i_copies + y_copies:
         copy.wait_send()
     for k in range(count):
         block_copy(k).wait_send()
@@ -359,20 +375,9 @@
             chain_copy(late, k).wait_send()
 
 
-def tap_matrix(width, rows_per):
-    half = width // 2
-    taps = np.zeros((half, width), np.float32)
-    for b in range(half):
-        for q in range(4):
-            taps[b, min(max(2 * b - 1 + q, 0), width - 1)] += cubic_taps[q]
-    return jnp.asarray(np.kron(np.eye(rows_per, dtype=np.float32), taps), jnp.bfloat16)
-
-
 def per_device(n, m, student, teacher):
     _, tokens, feats = student.shape
     _, height, width, _ = teacher.shape
-    rows_per = max(1, 256 // width)
-    groups = height // rows_per
     nb = tokens // BLOCK
     half = nb // 2 + nb * (nb - 1) // 4
     count = half * SPLIT
@@ -390,7 +395,6 @@
         in_specs=[
             pl.BlockSpec(memory_space=pl.ANY),
             pl.BlockSpec(memory_space=pl.ANY),
-            pl.BlockSpec(memory_space=pltpu.VMEM),
         ],
         out_specs=(
             pl.BlockSpec(memory_space=pltpu.VMEM),
@@ -398,16 +402,16 @@
         ),
         scratch_shapes=[
             vmem((tokens, feats), bf16),
-            vmem((height, width, feats), bf16),
-            vmem((height + 2, width // 2, feats), f32),
+            vmem((height + 2, width, feats), bf16),
+            vmem((UNROLL, feats // LANES, width + 16, LANES), f32),
             vmem((tokens, feats), f32),
             vmem((tokens, feats), bf16),
             vmem((tokens, feats), bf16),
             vmem((tokens, LANES), f32),
             vmem((tokens, LANES), f32),
             vmem((tokens, LANES), f32),
-            vmem((n, tiles, LANES), f32),
-            vmem((n, tiles, LANES), f32),
+            vmem((tokens, LANES), f32),
+            vmem((n, 2 * tiles, LANES), f32),
             vmem((n, tiles, LANES), f32),
             vmem((n, 8, LANES), f32),
             vmem((m, 8, LANES), f32),
@@ -421,8 +425,8 @@
             vmem((tokens, tokens), bf16),
             vmem((tokens, feats), f32),
             vmem((1, BLOCK), f32),
-            dma((groups + 1,)),
-            dma((n - 1,)), dma((n - 1,)), dma((n - 1,)), dma((n - 1,)),
+            dma((CHUNKS + 3,)),
+            dma((n - 1,)), dma((n - 1,)),
             dma((n - 1,)), dma((n - 1,)), dma((n - 1,)), dma((n - 1,)),
             dma((m - 1,)), dma((m - 1,)),
             dma((count,)), dma((count,)),
@@ -432,7 +436,7 @@
         compiler_params=pltpu.CompilerParams(
             collective_id=0, has_side_effects=True, vmem_limit_bytes=56 * 1024 * 1024
         ),
-    )(student, teacher, tap_matrix(width, rows_per))
+    )(student, teacher)
     return gradient, loss[0, 0]
 
 

time: 58.1 us -> 55.2 us (0.950)
  Pallas kernels: 53.8 us -> 50.9 us
    pallas_call x1, Pallas kernels: 53.8 us -> 50.9 us  [per_device(): pl.pallas_call(functools.partial(kernel, (n, m)), name='anchor', out_shap...]
where the time goes in v1:
time: 55.2 us; the launch traced here: 55 us
  Pallas kernels  50.9 us (92%)
  local copies, waits for them, and re-layouts  3.45 us (6%)
  between operations  0.64 us (1%)
    pallas_call x1, Pallas kernels, per_device(): pl.pallas_call(functools.partial(kernel, (n, m)), name='anchor', out_shap...  50.9 us
    unnamed x1, local copies, waits for them, and re-layouts  2.26 us
    slice x1, local copies, waits for them, and re-layouts, per_device(): return (gradient, loss[0, 0])  1.19 us

profile of v1, /device:TPU:0, one launch (start us, length us, event | category | flops | bytes accessed | tf_op | source)
XLA Modules:
  0.0 55.0 jit_solution(3685181948967045668)
XLA Ops:
  0.6 50.9 %anchor.1 = (bf16[1,1024,512]{2,1,0:T(8,128)(2,1)}, f32[8,128]{1,0:T(8,128)}) custom-call(bf16[1,1024,512]{2,1,0:T(8,128)(2,1)} %student_hbm.1, bf16[1,64,64,512]{3,2,1,0:T(8,128)(2,1)} %teacher_hbm.1), custom_call_target="tpu_custom_call" | custom-call | tf_op jit(solution)/shard_map/anchor/pallas_call | solution.py:388
  51.5 1.2 %slice.3 = f32[1,1]{1,0:T(1,128)} slice(f32[8,128]{1,0:T(8,128)} %get-tuple-element.5), slice={[0:1], [0:1]} | slice | bytes 8 | tf_op jit(solution)/shard_map/slice | solution.py:440
  52.7 2.3 %copy.5 = bf16[1,1024,512]{2,1,0:T(8,128)(2,1)} copy(bf16[1,1024,512]{2,1,0:T(8,128)(2,1)} %get-tuple-element.8) | data formatting | bytes 2097152

commit v2 on v1

v2 whole, which is shorter than its diff:
```python
import functools

import jax
import jax.numpy as jnp
from jax import lax
from jax.experimental import pallas as pl
from jax.experimental.pallas import tpu as pltpu
from jax.sharding import PartitionSpec as P

cubic_taps = (-0.09375, 0.59375, 0.59375, -0.09375)
epsilon = 1e-06
LANES = 128
BLOCK = 256
HALF = BLOCK // 2
PIECE = 64
END_LAG = 14
END_GAP = 4
MID_LAG = 5
MID_GAP = 8
OUT_CHUNKS = 4
CHUNKS = 4
UNROLL = 2


def lane_tiles_sum(x):
    total = x[:, :LANES]
    for start in range(LANES, x.shape[1], LANES):
        total = total + x[:, start : start + LANES]
    return total


def spread(column, width):
    return jnp.concatenate([column] * (width // LANES), axis=1)


def plan(nb):
    upper = [(i, j) for i in range(nb) for j in range(i + 1, nb)]
    return upper, len(upper) // 2, nb // 2, BLOCK // PIECE, HALF // PIECE


def kernel(
    sizes, student_hbm, teacher_hbm, sbuf, pull, inv, tinv, loss_ref,
    tbuf, vbuf, shrunk, unit_low, teach_low, part, tpart,
    norms, diags, along, img_losses,
    own, prefix, ysend, yrecv, zin, zout, gathered, sqacc,
    load_sem, s_send, s_recv, d_send, d_recv, a_send, a_recv,
    i_send, i_recv, y_send, y_recv, z_send, z_recv, g_send, g_recv,
):
    n, m = sizes
    tokens, feats = unit_low.shape
    height, width = tbuf.shape[0] - 2, tbuf.shape[1]
    half_w = width // 2
    lane_tiles = feats // LANES
    nb = tokens // BLOCK
    tiles = tokens // LANES
    me = lax.axis_index("tok")
    img = lax.axis_index("img")
    col = lax.rem(me, 2)
    row = me // 2
    chain = n // 2
    upper, offs, diag, per_off, per_diag = plan(nb)
    corners = diag * per_diag
    count = corners + offs * per_off
    early = jnp.where(row < (chain + 1) // 2, 0, 1)
    late = 1 - early
    rank = jnp.minimum(row, chain - 1 - row)

    student_load = pltpu.make_async_copy(student_hbm.at[0], sbuf, load_sem.at[0])
    student_load.start()

    def load(index, first, last, to):
        copy = pltpu.make_async_copy(
            teacher_hbm.at[0, first:last],
            tbuf.at[to : to + last - first],
            load_sem.at[index],
        )
        copy.start()
        return copy

    step = height // CHUNKS
    top = load(1, 0, 1, 0)
    loads = []
    for q in range(CHUNKS):
        first = q * step + 1 if q else 0
        last = height if q == CHUNKS - 1 else (q + 1) * step + 1
        loads.append(load(3 + q, first, last, first + 1))
    bottom = load(2, height - 1, height, height + 1)

    barrier = pltpu.get_barrier_semaphore()
    for p in range(1, n):
        pl.semaphore_signal(barrier, 1, device_id={"tok": lax.rem(me + p, n)})
    for p in range(1, m):
        pl.semaphore_signal(barrier, 1, device_id={"img": lax.rem(img + p, m)})

    def gather_copies(buf, send, recv, axis, here, size):
        return [
            pltpu.make_async_remote_copy(
                src_ref=buf.at[here],
                dst_ref=buf.at[here],
                send_sem=send.at[p - 1],
                recv_sem=recv.at[p - 1],
                device_id={axis: lax.rem(here + p, size)},
            )
            for p in range(1, size)
        ]

    def pack_rows(sources):
        lane = lax.broadcasted_iota(jnp.int32, (LANES, LANES), 1)
        columns = jnp.zeros((LANES, LANES), jnp.float32)
        for k, source in enumerate(sources):
            for b in range(tiles):
                block = source[b * LANES : (b + 1) * LANES, :]
                total = jnp.sum(block, axis=1, keepdims=True)
                columns = jnp.where(lane == k * tiles + b, total, columns)
        return columns.T[: len(sources) * tiles]

    def summed(buf, size):
        total = buf[0]
        for k in range(1, size):
            total = total + buf[k]
        return total

    def unpack_rows(values, targets):
        blank = jnp.zeros((LANES - values.shape[0], LANES), jnp.float32)
        columns = jnp.concatenate([values, blank], axis=0).T
        for k, target in enumerate(targets):
            for b in range(tiles):
                at = k * tiles + b
                target[b * LANES : (b + 1) * LANES, :] = jnp.broadcast_to(
                    columns[:, at : at + 1], (LANES, LANES)
                )

    def slab(b):
        return pl.ds(pl.multiple_of(b * LANES, LANES), LANES)

    @pl.when(rank == 0)
    def _():
        zin[early] = jnp.zeros(zin.shape[1:], zin.dtype)

    sqacc[...] = jnp.zeros_like(sqacc)
    pull[...] = jnp.zeros_like(pull)
    student_load.wait()

    @pl.loop(0, tiles)
    def _(b):
        x = sbuf[slab(b), :].astype(jnp.float32)
        part[slab(b), :] = lane_tiles_sum(x * x)

    def shrink_pair(first):
        for u in range(UNROLL):
            a = first * UNROLL + u
            x = [tbuf[2 * a + k].astype(jnp.float32) for k in range(4)]
            v = cubic_taps[1] * (x[1] + x[2]) + cubic_taps[0] * (x[0] + x[3])
            for t in range(lane_tiles):
                tile = v[:, t * LANES : (t + 1) * LANES]
                vbuf[u, t, 8 : 8 + width, :] = tile
                vbuf[u, t, 7:8, :] = tile[0:1]
                vbuf[u, t, 8 + width : 9 + width, :] = tile[width - 1 : width]
        for u in range(UNROLL):
            a = first * UNROLL + u
            rows = pl.ds(pl.multiple_of(a * half_w, half_w), half_w)
            total = None
            for t in range(lane_tiles):
                w = [vbuf[u, t, pl.ds(7 + k, half_w, stride=2), :] for k in range(4)]
                h = cubic_taps[1] * (w[1] + w[2]) + cubic_taps[0] * (w[0] + w[3])
                shrunk[rows, t * LANES : (t + 1) * LANES] = h
                total = h * h if total is None else total + h * h
            tpart[rows, :] = total

    top.wait()
    for q in range(CHUNKS):
        loads[q].wait()
        if q == CHUNKS - 1:
            bottom.wait()
        trips = step // 2 // UNROLL
        pl.loop(q * trips, (q + 1) * trips)(shrink_pair)

    norms[me] = pack_rows((part, tpart))
    pl.semaphore_wait(barrier, n - 1 + m - 1)
    s_copies = gather_copies(norms, s_send, s_recv, "tok", me, n)
    for copy in s_copies:
        copy.start()
    for copy in s_copies:
        copy.wait_recv()
    unpack_rows(lax.rsqrt(summed(norms, n) + epsilon), (inv, tinv))

    @pl.loop(0, tiles)
    def _(b):
        x = sbuf[slab(b), :].astype(jnp.float32) * spread(inv[slab(b), :], feats)
        y = shrunk[slab(b), :] * spread(tinv[slab(b), :], feats)
        shrunk[slab(b), :] = x
        x = x.astype(jnp.bfloat16)
        unit_low[slab(b), :] = x
        y = y.astype(jnp.bfloat16)
        teach_low[slab(b), :] = y
        x = x.astype(jnp.float32)
        y = y.astype(jnp.float32)
        part[slab(b), :] = lane_tiles_sum(x * x - y * y)

    def strip(i):
        return pl.ds(pl.multiple_of(i * BLOCK, BLOCK), BLOCK)

    def gram(i, j):
        def product(low):
            return lax.dot_general(
                low[strip(i), :], low[strip(j), :], (((1,), (1,)), ((), ())),
                preferred_element_type=jnp.float32,
            )

        return product(unit_low) - product(teach_low)

    def pick(first, second, c):
        return tuple(p + c * (q - p) for p, q in zip(first, second))

    def off_block(k, c):
        return pick(upper[k], upper[offs + k], c)

    def diag_block(k, c):
        return 2 * k + c

    row_at = lax.broadcasted_iota(jnp.int32, (HALF, HALF), 0)
    col_at = lax.broadcasted_iota(jnp.int32, (HALF, HALF), 1)

    def fold(block):
        corner = jnp.where(row_at < col_at, block[:HALF, :HALF], block[HALF:, HALF:])
        return jnp.concatenate([corner, block[:HALF, HALF:]], axis=1)

    def y_copy(k):
        return pltpu.make_async_remote_copy(
            src_ref=ysend.at[k], dst_ref=yrecv.at[k],
            send_sem=y_send.at[k], recv_sem=y_recv.at[k],
            device_id={"tok": me + 1 - 2 * col},
        )

    def share(k, c):
        if k < diag:
            i = diag_block(k, c)
            return fold(gram(i, i)), k * per_diag, per_diag
        return gram(*off_block(k - diag, c)), corners + (k - diag) * per_off, per_off

    def give(k):
        block, first, amount = share(k, 1 - col)
        block = block.astype(jnp.bfloat16)
        for t in range(amount):
            ysend[first + t] = block[t * PIECE : (t + 1) * PIECE]
            y_copy(first + t).start()

    def keep(k):
        block, first, amount = share(k, col)
        own[first : first + amount] = block.reshape(amount, PIECE, BLOCK)

    def hop(direction):
        return {"tok": lax.rem(me + 2 - 4 * direction + n, n)}

    for k in range(offs + diag):
        give(k)
    for k in range(offs + diag):
        keep(k)
    diags[me] = pack_rows((part,))
    part[...] = jnp.zeros_like(part)
    d_copies = gather_copies(diags, d_send, d_recv, "tok", me, n)
    for copy in d_copies:
        copy.start()

    def chain_copy(direction, k):
        return pltpu.make_async_remote_copy(
            src_ref=zout.at[direction, k], dst_ref=zin.at[direction, k],
            send_sem=z_send.at[direction, k], recv_sem=z_recv.at[direction, k],
            device_id=hop(direction),
        )

    def accumulate(i, j, block):
        product = jnp.dot(block, unit_low[strip(j), :], preferred_element_type=jnp.float32)
        rows = strip(i)
        pull[rows, :] += product
        part[rows, :] += lane_tiles_sum(shrunk[rows, :] * product)

    def unfold(i, block):
        corner = block[:, :HALF].astype(jnp.float32)
        turned = corner.T
        diagonal = summed_diag(i)
        side = block[:, HALF:]

        def whole(above, below, middle):
            value = jnp.where(row_at < col_at, above, below)
            return jnp.where(row_at == col_at, middle, value).astype(jnp.bfloat16)

        top = jnp.concatenate([whole(corner, turned, diagonal[0]), side], axis=1)
        side = side.astype(jnp.float32).T.astype(jnp.bfloat16)
        low = jnp.concatenate([side, whole(turned, corner, diagonal[1])], axis=1)
        return jnp.concatenate([top, low], axis=0)

    def jobs(k, c, owner):
        amount = per_diag if k < corners else per_off
        at = k if k < corners else k - corners
        if at % amount < amount - 1:
            return []

        def block():
            rows = gathered[owner, k - amount + 1 : k + 1]
            return rows.reshape(amount * PIECE, BLOCK)

        if k < corners:
            i = diag_block(at // amount, c)
            return [lambda: accumulate(i, i, unfold(i, block()))]
        i, j = off_block(at // amount, c)
        return [
            lambda: accumulate(i, j, block()),
            lambda: accumulate(j, i, block().T),
        ]

    def summed_diag(i):
        values = []
        for t in range(2):
            total = diags[0, pl.ds(2 * i + t, 1), :]
            for k in range(1, n):
                total = total + diags[k, pl.ds(2 * i + t, 1), :]
            values.append(jnp.broadcast_to(total, (HALF, HALF)))
        return values

    def block_copy(k):
        return pltpu.make_async_remote_copy(
            src_ref=gathered.at[0, k], dst_ref=gathered.at[1, k],
            send_sem=g_send.at[k], recv_sem=g_recv.at[k],
            device_id={"tok": me + 1 - 2 * col},
        )

    def count_squares(total):
        sqacc[...] += 2.0 * jnp.sum(total * total, axis=0, keepdims=True)

    def run_early(k):
        y_copy(k).wait_recv()
        mine = own[k] + yrecv[k].astype(jnp.float32)
        copy = chain_copy(early, k)

        @pl.when(rank > 0)
        def _():
            copy.wait_recv()

        total = mine + zin[early, k].astype(jnp.float32)
        zout[early, k] = total.astype(jnp.bfloat16)
        own[k] = mine
        prefix[k] = total
        copy.start()

    def run_late(k):
        copy = chain_copy(late, k)
        copy.wait_recv()
        incoming = zin[late, k].astype(jnp.float32)
        total = prefix[k] + incoming

        @pl.when(rank > 0)
        def _():
            zout[late, k] = (own[k] + incoming).astype(jnp.bfloat16)
            copy.start()

        gathered[0, k] = total.astype(jnp.bfloat16)
        block_copy(k).start()
        if k < corners:
            first = (k % per_diag) * PIECE
            on_diagonal = row_at[:PIECE] + first == col_at[:PIECE]
            corner = jnp.where(on_diagonal, 0.0, total[:, :HALF])
            total = jnp.concatenate([corner, total[:, HALF:]], axis=1)
            if k % per_diag == 0:
                for value in summed_diag(diag_block(k // per_diag, col)):
                    sqacc[:, :HALF] += value[:1] * value[:1]
        count_squares(total)

    def run_other(k):
        block_copy(k).wait_recv()

    def await_diags():
        for copy in d_copies:
            copy.wait_recv()

    i_copies = gather_copies(img_losses, i_send, i_recv, "img", img, m)

    def send_losses():
        squared = jnp.sum(sqacc[...], axis=1, keepdims=True)
        img_losses[img] = jnp.broadcast_to(squared, img_losses.shape[1:])
        for copy in i_copies:
            copy.start()

    def run(lag, gap):
        waiting = []
        for k in range(count + lag + gap):
            if k < count:
                run_early(k)
            if k == lag:
                await_diags()
            if lag <= k < count + lag:
                run_late(k - lag)
                waiting += jobs(k - lag, col, 0)
            if k == count + lag - 1:
                send_losses()
            if lag + gap <= k:
                run_other(k - lag - gap)
                waiting += jobs(k - lag - gap, 1 - col, 1)
            if waiting:
                waiting.pop(0)()
        for job in waiting:
            job()

    @pl.when(rank == 0)
    def _():
        run(END_LAG, END_GAP)

    @pl.when(rank > 0)
    def _():
        run(MID_LAG, MID_GAP)

    for copy in i_copies:
        copy.wait_recv()
    along[me, :tiles] = pack_rows((part,))
    along[me, tiles:] = summed(img_losses, m)
    a_copies = gather_copies(along, a_send, a_recv, "tok", me, n)
    for copy in a_copies:
        copy.start()
    for copy in a_copies:
        copy.wait_recv()
    total = summed(along, n)
    unpack_rows(total[:tiles], (tinv,))
    loss_ref[...] = total[tiles:] / (chain * tokens)

    for copy in s_copies + d_copies + a_copies + i_copies:
        copy.wait_send()
    for k in range(count):
        y_copy(k).wait_send()
        block_copy(k).wait_send()
        chain_copy(early, k).wait_send()

        @pl.when(rank > 0)
        def _():
            chain_copy(late, k).wait_send()


def finish(student_ref, pull_ref, inv_ref, along_ref, loss_ref, out_hbm, total_ref, buf, sem):
    tokens, feats = pull_ref.shape
    rows = tokens // OUT_CHUNKS
    copies = []
    for b in range(OUT_CHUNKS):
        at = pl.ds(b * rows, rows)
        scale = spread(inv_ref[at, :], feats)
        unit = student_ref[at, :].astype(jnp.float32) * scale
        grad = scale * (4.0 * pull_ref[at, :])
        grad = grad - scale * unit * spread(4.0 * along_ref[at, :], feats)
        buf[at, :] = grad.astype(buf.dtype)
        copy = pltpu.make_async_copy(buf.at[at], out_hbm.at[0, at], sem.at[b])
        copy.start()
        copies.append(copy)
    total_ref[...] = loss_ref[0:1, 0:1]
    for copy in copies:
        copy.wait()


def per_device(n, m, student, teacher):
    _, tokens, feats = student.shape
    _, height, width, _ = teacher.shape
    nb = tokens // BLOCK
    _, offs, diag, per_off, per_diag = plan(nb)
    count = offs * per_off + diag * per_diag
    tiles = tokens // LANES
    f32, bf16 = jnp.float32, jnp.bfloat16
    vmem, dma = pltpu.VMEM, pltpu.SemaphoreType.DMA
    features, pull, inv, along, loss = pl.pallas_call(
        functools.partial(kernel, (n, m)),
        name="anchor",
        out_shape=(
            jax.ShapeDtypeStruct((tokens, feats), bf16),
            jax.ShapeDtypeStruct((tokens, feats), f32),
            jax.ShapeDtypeStruct((tokens, LANES), f32),
            jax.ShapeDtypeStruct((tokens, LANES), f32),
            jax.ShapeDtypeStruct((8, LANES), f32),
        ),
        in_specs=[
            pl.BlockSpec(memory_space=pltpu.HBM),
            pl.BlockSpec(memory_space=pltpu.HBM),
        ],
        out_specs=(pl.BlockSpec(memory_space=pltpu.VMEM),) * 5,
        scratch_shapes=[
            vmem((height + 2, width, feats), bf16),
            vmem((UNROLL, feats // LANES, width + 16, LANES), f32),
            vmem((tokens, feats), f32),
            vmem((tokens, feats), bf16),
            vmem((tokens, feats), bf16),
            vmem((tokens, LANES), f32),
            vmem((tokens, LANES), f32),
            vmem((n, 2 * tiles, LANES), f32),
            vmem((n, tiles, LANES), f32),
            vmem((n, tiles + 8, LANES), f32),
            vmem((m, 8, LANES), f32),
            vmem((count, PIECE, BLOCK), f32),
            vmem((count, PIECE, BLOCK), f32),
            vmem((count, PIECE, BLOCK), bf16),
            vmem((count, PIECE, BLOCK), bf16),
            vmem((2, count, PIECE, BLOCK), bf16),
            vmem((2, count, PIECE, BLOCK), bf16),
            vmem((2, count, PIECE, BLOCK), bf16),
            vmem((1, BLOCK), f32),
            dma((CHUNKS + 3,)),
            dma((n - 1,)), dma((n - 1,)), dma((n - 1,)), dma((n - 1,)),
            dma((n - 1,)), dma((n - 1,)),
            dma((m - 1,)), dma((m - 1,)),
            dma((count,)), dma((count,)),
            dma((2, count)), dma((2, count)),
            dma((count,)), dma((count,)),
        ],
        compiler_params=pltpu.CompilerParams(
            collective_id=0, has_side_effects=True, vmem_limit_bytes=32 * 1024 * 1024
        ),
    )(*(pltpu.with_memory_space_constraint(x, pltpu.HBM) for x in (student, teacher)))
    gradient, total = pl.pallas_call(
        finish,
        name="finish",
        out_shape=(
            jax.ShapeDtypeStruct(student.shape, bf16),
            jax.ShapeDtypeStruct((1, 1), f32),
        ),
        in_specs=[pl.BlockSpec(memory_space=pltpu.VMEM)] * 5,
        out_specs=(
            pl.BlockSpec(memory_space=pl.ANY),
            pl.BlockSpec(memory_space=pltpu.VMEM),
        ),
        scratch_shapes=[vmem((tokens, feats), bf16), dma((OUT_CHUNKS,))],
        compiler_params=pltpu.CompilerParams(vmem_limit_bytes=16 * 1024 * 1024),
    )(features, pull, inv, along, loss)
    return gradient, total.reshape(())


def solution(mesh):
    return jax.shard_map(
        functools.partial(per_device, mesh.shape["tok"], mesh.shape["img"]),
        mesh=mesh,
        in_specs=(P("img", None, "tok"), P("img", None, None, "tok")),
        out_specs=(P("img", None, "tok"), P()),
        check_vma=False,
    )
```

time: 55.2 us -> 51.2 us (0.928)
  local copies, waits for them, and re-layouts: 3.45 us -> 0 us
    pallas_call x1, Pallas kernels: 50.9 us -> 48.6 us  [per_device(): pl.pallas_call(functools.partial(kernel, (n, m)), name='anchor', out_shap...]
    unnamed x1 -> x0, local copies, waits for them, and re-layouts: 2.26 us -> none
    pallas_call x0 -> x1, Pallas kernels: none -> 1.78 us  [per_device(): pl.pallas_call(finish, name='finish', out_shape=(jax.ShapeDtypeStruct(stu...]
    slice x1 -> x0, local copies, waits for them, and re-layouts: 1.19 us -> none  [per_device(): return (gradient, loss[0, 0])]
where the time goes in v2:
time: 51.2 us; the launch traced here: 51 us
  Pallas kernels  50.4 us (98%)
  between operations  0.64 us (1%)
    pallas_call x1, Pallas kernels, per_device(): pl.pallas_call(functools.partial(kernel, (n, m)), name='anchor', out_shap...  48.6 us
    pallas_call x1, Pallas kernels, per_device(): pl.pallas_call(finish, name='finish', out_shape=(jax.ShapeDtypeStruct(stu...  1.78 us

profile of v2, /device:TPU:0, one launch (start us, length us, event | category | flops | bytes accessed | tf_op | source)
XLA Modules:
  0.0 51.0 jit_solution(17081712489457843136)
XLA Ops:
  0.6 48.6 %anchor.1 = (bf16[1024,512]{1,0:T(8,128)(2,1)S(1)}, f32[1024,512]{1,0:T(8,128)S(1)}, f32[1024,128]{1,0:T(8,128)S(1)}, f32[1024,128]{1,0:T(8,128)S(1)}, f32[8,128]{1,0:T(8,128)S(1)}) custom-call(bf16[1,1024,512]{2,1,0:T(8,128)(2,1)} %student_hbm.1, bf16[1,64,64,512]{3,2,1,0:T(8,128)(2,1)} %teacher_hbm.1), custom_call_target="tpu_custom_call" | custom-call | tf_op jit(solution)/shard_map/anchor/pallas_call | solution.py:465
  49.2 1.8 %finish.1 = (bf16[1,1024,512]{2,1,0:T(8,128)(2,1)}, f32[1,1]{1,0:T(1,128)}) custom-call(bf16[1024,512]{1,0:T(8,128)(2,1)S(1)} %get-tuple-element.9.student_ref, f32[1024,512]{1,0:T(8,128)S(1)} %get-tuple-element.10.pull_ref, f32[1024,128]{1,0:T(8,128)S(1)} %get-tuple-element.11.inv_ref, f32[1024,128]{1,0:T(8,128)S(1)} %get-tuple-element.12.along_ref, ...), custom_call_target="tpu_custom_call" | custom-call | tf_op jit(solution)/shard_map/finish/pallas_call | solution.py:512

commit v3 on v2

--- a/solution.py
+++ b/solution.py
@@ -14,10 +14,11 @@
 HALF = BLOCK // 2
 PIECE = 64
 END_LAG = 14
-END_GAP = 4
+END_GAP = 6
 MID_LAG = 5
 MID_GAP = 8
 OUT_CHUNKS = 4
+GROUPS = 2
 CHUNKS = 4
 UNROLL = 2
 
@@ -34,8 +35,13 @@
 
 
 def plan(nb):
-    upper = [(i, j) for i in range(nb) for j in range(i + 1, nb)]
-    return upper, len(upper) // 2, nb // 2, BLOCK // PIECE, HALF // PIECE
+    blocks, first, count = [], [], 0
+    for j in range(nb):
+        for i in [j] + list(range(j)):
+            blocks.append((i, j))
+            first.append(count)
+            count += (HALF if i < j else HALF // 2) // PIECE
+    return blocks, first + [count]
 
 
 def kernel(
@@ -58,33 +64,33 @@
     col = lax.rem(me, 2)
     row = me // 2
     chain = n // 2
-    upper, offs, diag, per_off, per_diag = plan(nb)
-    corners = diag * per_diag
-    count = corners + offs * per_off
+    blocks, first = plan(nb)
+    count = first[-1]
     early = jnp.where(row < (chain + 1) // 2, 0, 1)
     late = 1 - early
     rank = jnp.minimum(row, chain - 1 - row)
 
-    student_load = pltpu.make_async_copy(student_hbm.at[0], sbuf, load_sem.at[0])
-    student_load.start()
-
-    def load(index, first, last, to):
-        copy = pltpu.make_async_copy(
-            teacher_hbm.at[0, first:last],
-            tbuf.at[to : to + last - first],
-            load_sem.at[index],
-        )
+    step, share = height // CHUNKS, tokens // CHUNKS
+
+    def load(index, src, dst):
+        copy = pltpu.make_async_copy(src, dst, load_sem.at[index])
         copy.start()
         return copy
 
-    step = height // CHUNKS
-    top = load(1, 0, 1, 0)
+    def load_teacher(index, low, high, to):
+        return load(index, teacher_hbm.at[0, low:high], tbuf.at[to : to + high - low])
+
+    top = load_teacher(0, 0, 1, 0)
     loads = []
     for q in range(CHUNKS):
-        first = q * step + 1 if q else 0
-        last = height if q == CHUNKS - 1 else (q + 1) * step + 1
-        loads.append(load(3 + q, first, last, first + 1))
-    bottom = load(2, height - 1, height, height + 1)
+        low = q * step + 1 if q else 0
+        high = height if q == CHUNKS - 1 else (q + 1) * step + 1
+        rows = slice(q * share, (q + 1) * share)
+        loads.append((
+            load_teacher(2 + 2 * q, low, high, low + 1),
+            load(3 + 2 * q, student_hbm.at[0, rows], sbuf.at[rows]),
+        ))
+    bottom = load_teacher(1, height - 1, height, height + 1)
 
     barrier = pltpu.get_barrier_semaphore()
     for p in range(1, n):
@@ -104,15 +110,15 @@
             for p in range(1, size)
         ]
 
-    def pack_rows(sources):
+    def pack_rows(sources, base, amount):
         lane = lax.broadcasted_iota(jnp.int32, (LANES, LANES), 1)
         columns = jnp.zeros((LANES, LANES), jnp.float32)
         for k, source in enumerate(sources):
-            for b in range(tiles):
-                block = source[b * LANES : (b + 1) * LANES, :]
+            for b in range(amount):
+                block = source[(base + b) * LANES : (base + b + 1) * LANES, :]
                 total = jnp.sum(block, axis=1, keepdims=True)
-                columns = jnp.where(lane == k * tiles + b, total, columns)
-        return columns.T[: len(sources) * tiles]
+                columns = jnp.where(lane == k * amount + b, total, columns)
+        return columns.T[: len(sources) * amount]
 
     def summed(buf, size):
         total = buf[0]
@@ -120,35 +126,28 @@
             total = total + buf[k]
         return total
 
-    def unpack_rows(values, targets):
+    def unpack_rows(values, targets, base, amount):
         blank = jnp.zeros((LANES - values.shape[0], LANES), jnp.float32)
         columns = jnp.concatenate([values, blank], axis=0).T
         for k, target in enumerate(targets):
-            for b in range(tiles):
-                at = k * tiles + b
-                target[b * LANES : (b + 1) * LANES, :] = jnp.broadcast_to(
+            for b in range(amount):
+                at = k * amount + b
+                target[(base + b) * LANES : (base + b + 1) * LANES, :] = jnp.broadcast_to(
                     columns[:, at : at + 1], (LANES, LANES)
                 )
 
     def slab(b):
         return pl.ds(pl.multiple_of(b * LANES, LANES), LANES)
 
-    @pl.when(rank == 0)
-    def _():
-        zin[early] = jnp.zeros(zin.shape[1:], zin.dtype)
-
     sqacc[...] = jnp.zeros_like(sqacc)
     pull[...] = jnp.zeros_like(pull)
-    student_load.wait()
-
-    @pl.loop(0, tiles)
-    def _(b):
+    def student_squares(b):
         x = sbuf[slab(b), :].astype(jnp.float32)
         part[slab(b), :] = lane_tiles_sum(x * x)
 
-    def shrink_pair(first):
+    def shrink_pair(pair):
         for u in range(UNROLL):
-            a = first * UNROLL + u
+            a = pair * UNROLL + u
             x = [tbuf[2 * a + k].astype(jnp.float32) for k in range(4)]
             v = cubic_taps[1] * (x[1] + x[2]) + cubic_taps[0] * (x[0] + x[3])
             for t in range(lane_tiles):
@@ -157,7 +156,7 @@
                 vbuf[u, t, 7:8, :] = tile[0:1]
                 vbuf[u, t, 8 + width : 9 + width, :] = tile[width - 1 : width]
         for u in range(UNROLL):
-            a = first * UNROLL + u
+            a = pair * UNROLL + u
             rows = pl.ds(pl.multiple_of(a * half_w, half_w), half_w)
             total = None
             for t in range(lane_tiles):
@@ -167,25 +166,30 @@
                 total = h * h if total is None else total + h * h
             tpart[rows, :] = total
 
+    span = tiles // GROUPS
+    per_group = CHUNKS // GROUPS
+    s_copies = []
     top.wait()
     for q in range(CHUNKS):
-        loads[q].wait()
+        loads[q][0].wait()
         if q == CHUNKS - 1:
             bottom.wait()
         trips = step // 2 // UNROLL
         pl.loop(q * trips, (q + 1) * trips)(shrink_pair)
-
-    norms[me] = pack_rows((part, tpart))
-    pl.semaphore_wait(barrier, n - 1 + m - 1)
-    s_copies = gather_copies(norms, s_send, s_recv, "tok", me, n)
-    for copy in s_copies:
-        copy.start()
-    for copy in s_copies:
-        copy.wait_recv()
-    unpack_rows(lax.rsqrt(summed(norms, n) + epsilon), (inv, tinv))
-
-    @pl.loop(0, tiles)
-    def _(b):
+        loads[q][1].wait()
+        pl.loop(q * share // LANES, (q + 1) * share // LANES)(student_squares)
+        if q % per_group == per_group - 1:
+            g = q // per_group
+            norms[g, me] = pack_rows((part, tpart), g * span, span)
+            if g == 0:
+                pl.semaphore_wait(barrier, n - 1 + m - 1)
+            s_copies.append(
+                gather_copies(norms.at[g], s_send.at[g], s_recv.at[g], "tok", me, n)
+            )
+            for copy in s_copies[g]:
+                copy.start()
+
+    def normalise(b):
         x = sbuf[slab(b), :].astype(jnp.float32) * spread(inv[slab(b), :], feats)
         y = shrunk[slab(b), :] * spread(tinv[slab(b), :], feats)
         shrunk[slab(b), :] = x
@@ -197,6 +201,13 @@
         y = y.astype(jnp.float32)
         part[slab(b), :] = lane_tiles_sum(x * x - y * y)
 
+    def await_norms(g):
+        for copy in s_copies[g]:
+            copy.wait_recv()
+        values = lax.rsqrt(summed(norms.at[g], n) + epsilon)
+        unpack_rows(values, (inv, tinv), g * span, span)
+        pl.loop(g * span, (g + 1) * span)(normalise)
+
     def strip(i):
         return pl.ds(pl.multiple_of(i * BLOCK, BLOCK), BLOCK)
 
@@ -209,15 +220,6 @@
 
         return product(unit_low) - product(teach_low)
 
-    def pick(first, second, c):
-        return tuple(p + c * (q - p) for p, q in zip(first, second))
-
-    def off_block(k, c):
-        return pick(upper[k], upper[offs + k], c)
-
-    def diag_block(k, c):
-        return 2 * k + c
-
     row_at = lax.broadcasted_iota(jnp.int32, (HALF, HALF), 0)
     col_at = lax.broadcasted_iota(jnp.int32, (HALF, HALF), 1)
 
@@ -232,31 +234,26 @@
             device_id={"tok": me + 1 - 2 * col},
         )
 
-    def share(k, c):
-        if k < diag:
-            i = diag_block(k, c)
-            return fold(gram(i, i)), k * per_diag, per_diag
-        return gram(*off_block(k - diag, c)), corners + (k - diag) * per_off, per_off
-
-    def give(k):
-        block, first, amount = share(k, 1 - col)
-        block = block.astype(jnp.bfloat16)
-        for t in range(amount):
-            ysend[first + t] = block[t * PIECE : (t + 1) * PIECE]
-            y_copy(first + t).start()
-
-    def keep(k):
-        block, first, amount = share(k, col)
-        own[first : first + amount] = block.reshape(amount, PIECE, BLOCK)
+    def give(b):
+        i, j = blocks[b]
+        block = gram(i, j)
+        if i == j:
+            block = fold(block)
+        low, high = first[b], first[b + 1]
+        own[:, low:high] = block.reshape(2, high - low, PIECE, BLOCK)
+        for k in range(low, high):
+            ysend[k] = own[1 - col, k].astype(jnp.bfloat16)
+            y_copy(k).start()
 
     def hop(direction):
         return {"tok": lax.rem(me + 2 - 4 * direction + n, n)}
 
-    for k in range(offs + diag):
-        give(k)
-    for k in range(offs + diag):
-        keep(k)
-    diags[me] = pack_rows((part,))
+    for g in range(GROUPS):
+        await_norms(g)
+        for b, (i, j) in enumerate(blocks):
+            if j * GROUPS // nb == g:
+                give(b)
+    diags[me] = pack_rows((part,), 0, tiles)
     part[...] = jnp.zeros_like(part)
     d_copies = gather_copies(diags, d_send, d_recv, "tok", me, n)
     for copy in d_copies:
@@ -290,20 +287,18 @@
         low = jnp.concatenate([side, whole(turned, corner, diagonal[1])], axis=1)
         return jnp.concatenate([top, low], axis=0)
 
-    def jobs(k, c, owner):
-        amount = per_diag if k < corners else per_off
-        at = k if k < corners else k - corners
-        if at % amount < amount - 1:
+    def jobs(k):
+        if k + 1 not in first:
             return []
+        b = first.index(k + 1) - 1
+        i, j = blocks[b]
 
         def block():
-            rows = gathered[owner, k - amount + 1 : k + 1]
-            return rows.reshape(amount * PIECE, BLOCK)
-
-        if k < corners:
-            i = diag_block(at // amount, c)
+            pieces = gathered[:, first[b] : first[b + 1]]
+            return pieces.reshape(-1, BLOCK)
+
+        if i == j:
             return [lambda: accumulate(i, i, unfold(i, block()))]
-        i, j = off_block(at // amount, c)
         return [
             lambda: accumulate(i, j, block()),
             lambda: accumulate(j, i, block().T),
@@ -320,7 +315,7 @@
 
     def block_copy(k):
         return pltpu.make_async_remote_copy(
-            src_ref=gathered.at[0, k], dst_ref=gathered.at[1, k],
+            src_ref=gathered.at[col, k], dst_ref=gathered.at[col, k],
             send_sem=g_send.at[k], recv_sem=g_recv.at[k],
             device_id={"tok": me + 1 - 2 * col},
         )
@@ -328,42 +323,42 @@
     def count_squares(total):
         sqacc[...] += 2.0 * jnp.sum(total * total, axis=0, keepdims=True)
 
-    def run_early(k):
+    def run_early(k, outer):
         y_copy(k).wait_recv()
-        mine = own[k] + yrecv[k].astype(jnp.float32)
+        mine = own[col, k] + yrecv[k].astype(jnp.float32)
         copy = chain_copy(early, k)
 
-        @pl.when(rank > 0)
-        def _():
+        total = mine
+        if outer:
             copy.wait_recv()
-
-        total = mine + zin[early, k].astype(jnp.float32)
+            total = mine + zin[early, k].astype(jnp.float32)
         zout[early, k] = total.astype(jnp.bfloat16)
-        own[k] = mine
+        own[col, k] = mine
         prefix[k] = total
         copy.start()
 
-    def run_late(k):
+    def run_late(k, outer):
         copy = chain_copy(late, k)
         copy.wait_recv()
         incoming = zin[late, k].astype(jnp.float32)
         total = prefix[k] + incoming
 
-        @pl.when(rank > 0)
-        def _():
-            zout[late, k] = (own[k] + incoming).astype(jnp.bfloat16)
+        if outer:
+            zout[late, k] = (own[col, k] + incoming).astype(jnp.bfloat16)
             copy.start()
 
-        gathered[0, k] = total.astype(jnp.bfloat16)
+        gathered[col, k] = total.astype(jnp.bfloat16)
         block_copy(k).start()
-        if k < corners:
-            first = (k % per_diag) * PIECE
-            on_diagonal = row_at[:PIECE] + first == col_at[:PIECE]
+        b = max(x for x in range(len(blocks)) if first[x] <= k)
+        i, j = blocks[b]
+        if i == j:
+            offset = col * (HALF // 2) + (k - first[b]) * PIECE
+            on_diagonal = row_at[:PIECE] + offset == col_at[:PIECE]
             corner = jnp.where(on_diagonal, 0.0, total[:, :HALF])
             total = jnp.concatenate([corner, total[:, HALF:]], axis=1)
-            if k % per_diag == 0:
-                for value in summed_diag(diag_block(k // per_diag, col)):
-                    sqacc[:, :HALF] += value[:1] * value[:1]
+            if k == first[b]:
+                for value in summed_diag(i):
+                    sqacc[:, :HALF] += 0.5 * value[:1] * value[:1]
         count_squares(total)
 
     def run_other(k):
@@ -381,21 +376,20 @@
         for copy in i_copies:
             copy.start()
 
-    def run(lag, gap):
+    def run(lag, gap, outer):
         waiting = []
         for k in range(count + lag + gap):
             if k < count:
-                run_early(k)
+                run_early(k, outer)
             if k == lag:
                 await_diags()
             if lag <= k < count + lag:
-                run_late(k - lag)
-                waiting += jobs(k - lag, col, 0)
+                run_late(k - lag, outer)
             if k == count + lag - 1:
                 send_losses()
             if lag + gap <= k:
                 run_other(k - lag - gap)
-                waiting += jobs(k - lag - gap, 1 - col, 1)
+                waiting += jobs(k - lag - gap)
             if waiting:
                 waiting.pop(0)()
         for job in waiting:
@@ -403,15 +397,15 @@
 
     @pl.when(rank == 0)
     def _():
-        run(END_LAG, END_GAP)
+        run(END_LAG, END_GAP, False)
 
     @pl.when(rank > 0)
     def _():
-        run(MID_LAG, MID_GAP)
+        run(MID_LAG, MID_GAP, True)
 
     for copy in i_copies:
         copy.wait_recv()
-    along[me, :tiles] = pack_rows((part,))
+    along[me, :tiles] = pack_rows((part,), 0, tiles)
     along[me, tiles:] = summed(img_losses, m)
     a_copies = gather_copies(along, a_send, a_recv, "tok", me, n)
     for copy in a_copies:
@@ -419,10 +413,10 @@
     for copy in a_copies:
         copy.wait_recv()
     total = summed(along, n)
-    unpack_rows(total[:tiles], (tinv,))
+    unpack_rows(total[:tiles], (tinv,), 0, tiles)
     loss_ref[...] = total[tiles:] / (chain * tokens)
 
-    for copy in s_copies + d_copies + a_copies + i_copies:
+    for copy in sum(s_copies, []) + d_copies + a_copies + i_copies:
         copy.wait_send()
     for k in range(count):
         y_copy(k).wait_send()
@@ -457,8 +451,7 @@
     _, tokens, feats = student.shape
     _, height, width, _ = teacher.shape
     nb = tokens // BLOCK
-    _, offs, diag, per_off, per_diag = plan(nb)
-    count = offs * per_off + diag * per_diag
+    count = plan(nb)[1][-1]
     tiles = tokens // LANES
     f32, bf16 = jnp.float32, jnp.bfloat16
     vmem, dma = pltpu.VMEM, pltpu.SemaphoreType.DMA
@@ -485,11 +478,11 @@
             vmem((tokens, feats), bf16),
             vmem((tokens, LANES), f32),
             vmem((tokens, LANES), f32),
-            vmem((n, 2 * tiles, LANES), f32),
+            vmem((GROUPS, n, 2 * tiles // GROUPS, LANES), f32),
             vmem((n, tiles, LANES), f32),
             vmem((n, tiles + 8, LANES), f32),
             vmem((m, 8, LANES), f32),
-            vmem((count, PIECE, BLOCK), f32),
+            vmem((2, count, PIECE, BLOCK), f32),
             vmem((count, PIECE, BLOCK), f32),
             vmem((count, PIECE, BLOCK), bf16),
             vmem((count, PIECE, BLOCK), bf16),
@@ -497,8 +490,8 @@
             vmem((2, count, PIECE, BLOCK), bf16),
             vmem((2, count, PIECE, BLOCK), bf16),
             vmem((1, BLOCK), f32),
-            dma((CHUNKS + 3,)),
-            dma((n - 1,)), dma((n - 1,)), dma((n - 1,)), dma((n - 1,)),
+            dma((2 * CHUNKS + 2,)),
+            dma((GROUPS, n - 1)), dma((GROUPS, n - 1)), dma((n - 1,)), dma((n - 1,)),
             dma((n - 1,)), dma((n - 1,)),
             dma((m - 1,)), dma((m - 1,)),
             dma((count,)), dma((count,)),

time: 51.2 us -> 48.2 us (0.941)
  Pallas kernels: 50.4 us -> 47.4 us
    pallas_call x1, Pallas kernels: 48.6 us -> 45.6 us  [per_device(): pl.pallas_call(functools.partial(kernel, (n, m)), name='anchor', out_shap...]
where the time goes in v3:
time: 48.2 us; the launch traced here: 48 us
  Pallas kernels  47.4 us (98%)
  between operations  0.64 us (1%)
    pallas_call x1, Pallas kernels, per_device(): pl.pallas_call(functools.partial(kernel, (n, m)), name='anchor', out_shap...  45.6 us
    pallas_call x1, Pallas kernels, per_device(): pl.pallas_call(finish, name='finish', out_shape=(jax.ShapeDtypeStruct(stu...  1.78 us

profile of v3, /device:TPU:0, one launch (start us, length us, event | category | flops | bytes accessed | tf_op | source)
XLA Modules:
  0.0 48.0 jit_solution(6945921047819711495)
XLA Ops:
  0.6 45.6 %anchor.1 = (bf16[1024,512]{1,0:T(8,128)(2,1)S(1)}, f32[1024,512]{1,0:T(8,128)S(1)}, f32[1024,128]{1,0:T(8,128)S(1)}, f32[1024,128]{1,0:T(8,128)S(1)}, f32[8,128]{1,0:T(8,128)S(1)}) custom-call(bf16[1,1024,512]{2,1,0:T(8,128)(2,1)} %student_hbm.1, bf16[1,64,64,512]{3,2,1,0:T(8,128)(2,1)} %teacher_hbm.1), custom_call_target="tpu_custom_call" | custom-call | tf_op jit(solution)/shard_map/anchor/pallas_call | solution.py:458
  46.2 1.8 %finish.1 = (bf16[1,1024,512]{2,1,0:T(8,128)(2,1)}, f32[1,1]{1,0:T(1,128)}) custom-call(bf16[1024,512]{1,0:T(8,128)(2,1)S(1)} %get-tuple-element.9.student_ref, f32[1024,512]{1,0:T(8,128)S(1)} %get-tuple-element.10.pull_ref, f32[1024,128]{1,0:T(8,128)S(1)} %get-tuple-element.11.inv_ref, f32[1024,128]{1,0:T(8,128)S(1)} %get-tuple-element.12.along_ref, ...), custom_call_target="tpu_custom_call" | custom-call | tf_op jit(solution)/shard_map/finish/pallas_call | solution.py:505

commit v4 on v3

--- a/solution.py
+++ b/solution.py
@@ -13,10 +13,11 @@
 BLOCK = 256
 HALF = BLOCK // 2
 PIECE = 64
-END_LAG = 14
+END_LAG = 16
 END_GAP = 6
 MID_LAG = 5
 MID_GAP = 8
+QUICK = 1
 OUT_CHUNKS = 4
 GROUPS = 2
 CHUNKS = 4
@@ -35,22 +36,23 @@
 
 
 def plan(nb):
-    blocks, first, count = [], [], 0
+    quick = [(0, j) for j in range(1, nb)][:QUICK]
+    blocks = list(quick)
     for j in range(nb):
-        for i in [j] + list(range(j)):
-            blocks.append((i, j))
-            first.append(count)
-            count += (HALF if i < j else HALF // 2) // PIECE
-    return blocks, first + [count]
+        blocks += [(i, j) for i in [j] + list(range(j)) if (i, j) not in quick]
+    first = [0]
+    for i, j in blocks:
+        first.append(first[-1] + (HALF if i < j else HALF // 2) // PIECE)
+    return blocks, first, len(quick)
 
 
 def kernel(
     sizes, student_hbm, teacher_hbm, sbuf, pull, inv, tinv, loss_ref,
     tbuf, vbuf, shrunk, unit_low, teach_low, part, tpart,
     norms, diags, along, img_losses,
-    own, prefix, ysend, yrecv, zin, zout, gathered, sqacc,
+    own, prefix, ysend, yrecv, qsend, qrecv, factors, zin, zout, gathered, sqacc,
     load_sem, s_send, s_recv, d_send, d_recv, a_send, a_recv,
-    i_send, i_recv, y_send, y_recv, z_send, z_recv, g_send, g_recv,
+    i_send, i_recv, y_send, y_recv, q_send, q_recv, z_send, z_recv, g_send, g_recv,
 ):
     n, m = sizes
     tokens, feats = unit_low.shape
@@ -64,11 +66,17 @@
     col = lax.rem(me, 2)
     row = me // 2
     chain = n // 2
-    blocks, first = plan(nb)
+    blocks, first, quick = plan(nb)
     count = first[-1]
     early = jnp.where(row < (chain + 1) // 2, 0, 1)
     late = 1 - early
     rank = jnp.minimum(row, chain - 1 - row)
+
+    barrier = pltpu.get_barrier_semaphore()
+    for p in range(1, n):
+        pl.semaphore_signal(barrier, 1, device_id={"tok": lax.rem(me + p, n)})
+    for p in range(1, m):
+        pl.semaphore_signal(barrier, 1, device_id={"img": lax.rem(img + p, m)})
 
     step, share = height // CHUNKS, tokens // CHUNKS
 
@@ -91,12 +99,6 @@
             load(3 + 2 * q, student_hbm.at[0, rows], sbuf.at[rows]),
         ))
     bottom = load_teacher(1, height - 1, height, height + 1)
-
-    barrier = pltpu.get_barrier_semaphore()
-    for p in range(1, n):
-        pl.semaphore_signal(barrier, 1, device_id={"tok": lax.rem(me + p, n)})
-    for p in range(1, m):
-        pl.semaphore_signal(barrier, 1, device_id={"img": lax.rem(img + p, m)})
 
     def gather_copies(buf, send, recv, axis, here, size):
         return [
@@ -163,6 +165,7 @@
                 w = [vbuf[u, t, pl.ds(7 + k, half_w, stride=2), :] for k in range(4)]
                 h = cubic_taps[1] * (w[1] + w[2]) + cubic_taps[0] * (w[0] + w[3])
                 shrunk[rows, t * LANES : (t + 1) * LANES] = h
+                teach_low[rows, t * LANES : (t + 1) * LANES] = h.astype(jnp.bfloat16)
                 total = h * h if total is None else total + h * h
             tpart[rows, :] = total
 
@@ -205,6 +208,7 @@
         for copy in s_copies[g]:
             copy.wait_recv()
         values = lax.rsqrt(summed(norms.at[g], n) + epsilon)
+        factors[g] = values
         unpack_rows(values, (inv, tinv), g * span, span)
         pl.loop(g * span, (g + 1) * span)(normalise)
 
@@ -234,12 +238,46 @@
             device_id={"tok": me + 1 - 2 * col},
         )
 
+    def half(i, c):
+        return pl.ds(pl.multiple_of(i * BLOCK + c * HALF, HALF), HALF)
+
+    def half_gram(low, i, j, c):
+        return lax.dot_general(
+            low[half(i, c), :], low[strip(j), :], (((1,), (1,)), ((), ())),
+            preferred_element_type=jnp.float32,
+        )
+
+    def quick_copy(b, s):
+        return pltpu.make_async_remote_copy(
+            src_ref=qsend.at[s, b], dst_ref=qrecv.at[s, b],
+            send_sem=q_send.at[s, b], recv_sem=q_recv.at[s, b],
+            device_id={"tok": me + 1 - 2 * col},
+        )
+
+    def scaled(b, t, s):
+        i, j = blocks[b]
+        column = (inv, tinv)[s]
+        start = i * BLOCK + col * HALF + t * PIECE
+        rows = pl.ds(pl.multiple_of(start, PIECE), PIECE)
+        tile = j * (BLOCK // LANES)
+        at = s * span + tile % span
+        across = [
+            factors[tile // span, at + x : at + x + 1, :] for x in range(BLOCK // LANES)
+        ]
+        values = qrecv[s, b, t * PIECE : (t + 1) * PIECE].astype(jnp.float32)
+        values = values * spread(column[rows, :], BLOCK)
+        return values * jnp.concatenate(across, axis=1)
+
     def give(b):
         i, j = blocks[b]
+        low, high = first[b], first[b + 1]
+        if b < quick:
+            block = half_gram(unit_low, i, j, col) - half_gram(teach_low, i, j, col)
+            own[col, low:high] = block.reshape(high - low, PIECE, BLOCK)
+            return
         block = gram(i, j)
         if i == j:
             block = fold(block)
-        low, high = first[b], first[b + 1]
         own[:, low:high] = block.reshape(2, high - low, PIECE, BLOCK)
         for k in range(low, high):
             ysend[k] = own[1 - col, k].astype(jnp.bfloat16)
@@ -248,11 +286,16 @@
     def hop(direction):
         return {"tok": lax.rem(me + 2 - 4 * direction + n, n)}
 
+    for b in range(quick):
+        for s, low in enumerate((sbuf, teach_low)):
+            qsend[s, b] = half_gram(low, *blocks[b], 1 - col).astype(jnp.bfloat16)
+            quick_copy(b, s).start()
+
     for g in range(GROUPS):
         await_norms(g)
-        for b, (i, j) in enumerate(blocks):
-            if j * GROUPS // nb == g:
-                give(b)
+        ready = [b for b, (i, j) in enumerate(blocks) if j * GROUPS // nb == g]
+        for b in sorted(ready, key=lambda b: b < quick):
+            give(b)
     diags[me] = pack_rows((part,), 0, tiles)
     part[...] = jnp.zeros_like(part)
     d_copies = gather_copies(diags, d_send, d_recv, "tok", me, n)
@@ -324,8 +367,16 @@
         sqacc[...] += 2.0 * jnp.sum(total * total, axis=0, keepdims=True)
 
     def run_early(k, outer):
-        y_copy(k).wait_recv()
-        mine = own[col, k] + yrecv[k].astype(jnp.float32)
+        if k < first[quick]:
+            b = max(x for x in range(quick) if first[x] <= k)
+            if k == first[b]:
+                for s in range(2):
+                    quick_copy(b, s).wait_recv()
+            t = k - first[b]
+            mine = own[col, k] + (scaled(b, t, 0) - scaled(b, t, 1))
+        else:
+            y_copy(k).wait_recv()
+            mine = own[col, k] + yrecv[k].astype(jnp.float32)
         copy = chain_copy(early, k)
 
         total = mine
@@ -418,8 +469,12 @@
 
     for copy in sum(s_copies, []) + d_copies + a_copies + i_copies:
         copy.wait_send()
+    for b in range(quick):
+        for s in range(2):
+            quick_copy(b, s).wait_send()
     for k in range(count):
-        y_copy(k).wait_send()
+        if k >= first[quick]:
+            y_copy(k).wait_send()
         block_copy(k).wait_send()
         chain_copy(early, k).wait_send()
 
@@ -451,7 +506,8 @@
     _, tokens, feats = student.shape
     _, height, width, _ = teacher.shape
     nb = tokens // BLOCK
-    count = plan(nb)[1][-1]
+    _, first, quick = plan(nb)
+    count = first[-1]
     tiles = tokens // LANES
     f32, bf16 = jnp.float32, jnp.bfloat16
     vmem, dma = pltpu.VMEM, pltpu.SemaphoreType.DMA
@@ -486,6 +542,9 @@
             vmem((count, PIECE, BLOCK), f32),
             vmem((count, PIECE, BLOCK), bf16),
             vmem((count, PIECE, BLOCK), bf16),
+            vmem((2, quick, HALF, BLOCK), bf16),
+            vmem((2, quick, HALF, BLOCK), bf16),
+            vmem((GROUPS, 2 * tiles // GROUPS, LANES), f32),
             vmem((2, count, PIECE, BLOCK), bf16),
             vmem((2, count, PIECE, BLOCK), bf16),
             vmem((2, count, PIECE, BLOCK), bf16),
@@ -495,6 +554,7 @@
             dma((n - 1,)), dma((n - 1,)),
             dma((m - 1,)), dma((m - 1,)),
             dma((count,)), dma((count,)),
+            dma((2, quick)), dma((2, quick)),
             dma((2, count)), dma((2, count)),
             dma((count,)), dma((count,)),
         ],

time: 48.2 us -> 47.5 us (0.985)
  Pallas kernels: 47.4 us -> 46.7 us
    pallas_call x1, Pallas kernels: 45.6 us -> 44.9 us  [per_device(): pl.pallas_call(functools.partial(kernel, (n, m)), name='anchor', out_shap...]
where the time goes in v4:
time: 47.5 us; the launch traced here: 47.3 us
  Pallas kernels  46.7 us (98%)
  between operations  0.64 us (1%)
    pallas_call x1, Pallas kernels, per_device(): pl.pallas_call(functools.partial(kernel, (n, m)), name='anchor', out_shap...  44.9 us
    pallas_call x1, Pallas kernels, per_device(): pl.pallas_call(finish, name='finish', out_shape=(jax.ShapeDtypeStruct(stu...  1.78 us

profile of v4, /device:TPU:0, one launch (start us, length us, event | category | flops | bytes accessed | tf_op | source)
XLA Modules:
  0.0 47.3 jit_solution(16894788812496855337)
XLA Ops:
  0.6 44.9 %anchor.1 = (bf16[1024,512]{1,0:T(8,128)(2,1)S(1)}, f32[1024,512]{1,0:T(8,128)S(1)}, f32[1024,128]{1,0:T(8,128)S(1)}, f32[1024,128]{1,0:T(8,128)S(1)}, f32[8,128]{1,0:T(8,128)S(1)}) custom-call(bf16[1,1024,512]{2,1,0:T(8,128)(2,1)} %student_hbm.1, bf16[1,64,64,512]{3,2,1,0:T(8,128)(2,1)} %teacher_hbm.1), custom_call_target="tpu_custom_call" | custom-call | tf_op jit(solution)/shard_map/anchor/pallas_call | solution.py:514
  45.5 1.8 %finish.1 = (bf16[1,1024,512]{2,1,0:T(8,128)(2,1)}, f32[1,1]{1,0:T(1,128)}) custom-call(bf16[1024,512]{1,0:T(8,128)(2,1)S(1)} %get-tuple-element.9.student_ref, f32[1024,512]{1,0:T(8,128)S(1)} %get-tuple-element.10.pull_ref, f32[1024,128]{1,0:T(8,128)S(1)} %get-tuple-element.11.inv_ref, f32[1024,128]{1,0:T(8,128)S(1)} %get-tuple-element.12.along_ref, ...), custom_call_target="tpu_custom_call" | custom-call | tf_op jit(solution)/shard_map/finish/pallas_call | solution.py:565

commit v5 on v4

--- a/solution.py
+++ b/solution.py
@@ -14,11 +14,11 @@
 HALF = BLOCK // 2
 PIECE = 64
 END_LAG = 16
-END_GAP = 6
+END_GAP = 8
 MID_LAG = 5
 MID_GAP = 8
 QUICK = 1
-OUT_CHUNKS = 4
+OUT_CHUNKS = 8
 GROUPS = 2
 CHUNKS = 4
 UNROLL = 2

time: 47.5 us -> 47.4 us (level)
  no operation moved by 1% of the time
where the time goes in v5:
time: 47.4 us; the launch traced here: 47.2 us
  Pallas kernels  46.6 us (98%)
  between operations  0.64 us (1%)
    pallas_call x1, Pallas kernels, per_device(): pl.pallas_call(functools.partial(kernel, (n, m)), name='anchor', out_shap...  44.8 us
    pallas_call x1, Pallas kernels, per_device(): pl.pallas_call(finish, name='finish', out_shape=(jax.ShapeDtypeStruct(stu...  1.77 us

profile of v5, /device:TPU:0, one launch (start us, length us, event | category | flops | bytes accessed | tf_op | source)
XLA Modules:
  0.0 47.2 jit_solution(6116060979145214710)
XLA Ops:
  0.6 44.8 %anchor.1 = (bf16[1024,512]{1,0:T(8,128)(2,1)S(1)}, f32[1024,512]{1,0:T(8,128)S(1)}, f32[1024,128]{1,0:T(8,128)S(1)}, f32[1024,128]{1,0:T(8,128)S(1)}, f32[8,128]{1,0:T(8,128)S(1)}) custom-call(bf16[1,1024,512]{2,1,0:T(8,128)(2,1)} %student_hbm.1, bf16[1,64,64,512]{3,2,1,0:T(8,128)(2,1)} %teacher_hbm.1), custom_call_target="tpu_custom_call" | custom-call | tf_op jit(solution)/shard_map/anchor/pallas_call | solution.py:514
  45.4 1.8 %finish.1 = (bf16[1,1024,512]{2,1,0:T(8,128)(2,1)}, f32[1,1]{1,0:T(1,128)}) custom-call(bf16[1024,512]{1,0:T(8,128)(2,1)S(1)} %get-tuple-element.9.student_ref, f32[1024,512]{1,0:T(8,128)S(1)} %get-tuple-element.10.pull_ref, f32[1024,128]{1,0:T(8,128)S(1)} %get-tuple-element.11.inv_ref, f32[1024,128]{1,0:T(8,128)S(1)} %get-tuple-element.12.along_ref, ...), custom_call_target="tpu_custom_call" | custom-call | tf_op jit(solution)/shard_map/finish/pallas_call | solution.py:565

commit v6 on v5

--- a/solution.py
+++ b/solution.py
@@ -21,7 +21,7 @@
 OUT_CHUNKS = 8
 GROUPS = 2
 CHUNKS = 4
-UNROLL = 2
+UNROLL = 4
 
 
 def lane_tiles_sum(x):

time: 47.4 us -> 47.3 us (level)
  no operation moved by 1% of the time
where the time goes in v6:
time: 47.3 us; the launch traced here: 47.2 us
  Pallas kernels  46.6 us (99%)
  between operations  0.64 us (1%)
    pallas_call x1, Pallas kernels, per_device(): pl.pallas_call(functools.partial(kernel, (n, m)), name='anchor', out_shap...  44.8 us
    pallas_call x1, Pallas kernels, per_device(): pl.pallas_call(finish, name='finish', out_shape=(jax.ShapeDtypeStruct(stu...  1.77 us

profile of v6, /device:TPU:0, one launch (start us, length us, event | category | flops | bytes accessed | tf_op | source)
XLA Modules:
  0.0 47.2 jit_solution(17333123698870802575)
XLA Ops:
  0.6 44.8 %anchor.1 = (bf16[1024,512]{1,0:T(8,128)(2,1)S(1)}, f32[1024,512]{1,0:T(8,128)S(1)}, f32[1024,128]{1,0:T(8,128)S(1)}, f32[1024,128]{1,0:T(8,128)S(1)}, f32[8,128]{1,0:T(8,128)S(1)}) custom-call(bf16[1,1024,512]{2,1,0:T(8,128)(2,1)} %student_hbm.1, bf16[1,64,64,512]{3,2,1,0:T(8,128)(2,1)} %teacher_hbm.1), custom_call_target="tpu_custom_call" | custom-call | tf_op jit(solution)/shard_map/anchor/pallas_call | solution.py:514
  45.4 1.8 %finish.1 = (bf16[1,1024,512]{2,1,0:T(8,128)(2,1)}, f32[1,1]{1,0:T(1,128)}) custom-call(bf16[1024,512]{1,0:T(8,128)(2,1)S(1)} %get-tuple-element.9.student_ref, f32[1024,512]{1,0:T(8,128)S(1)} %get-tuple-element.10.pull_ref, f32[1024,128]{1,0:T(8,128)S(1)} %get-tuple-element.11.inv_ref, f32[1024,128]{1,0:T(8,128)S(1)} %get-tuple-element.12.along_ref, ...), custom_call_target="tpu_custom_call" | custom-call | tf_op jit(solution)/shard_map/finish/pallas_call | solution.py:565
